TPU v7x, 256 devices: a whole 4x4x8 slice. The times are simulated.
256 devices in a mesh: rows: 4 (over y), cand: 64 (over x, z, core).
Axes of the slice: x: 4, y: 4, z: 8, core: 2. Of those that a mesh axis runs over, the one named last changes fastest.
Arguments:
- whitened: float32 [256, 2048], P('cand', 'rows'), may hold values from -6 to 6
- factor_rows: float32 [2048, 2048], P('rows'), as said below
- diag_inv: float32 [2048, 512], P('rows'), as said below
- observed: float32 [22, 2048], P(None, 'rows'), may hold values from 0 to 1
- inv_length: float32 [22], replicated, may hold values from 0.4 to 2
- grid_coords: int32 [22, 262144], P(None, 'cand'), may hold values from 0 to 20
- frequencies: float32 [22, 8192], P(None, 'rows'), may hold values from -8 to 8
- phases: float32 [8192], P('rows'), may hold values from -3.140625 to 3.140625
- prior_coef: bfloat16 [256, 8192], P('cand', 'rows'), may hold values from -6 to 6
Outputs:
- samples_at: float32 [262144, 256], P('cand', 'rows')
Inputs may be any that keep to these rules, and one draw needn't show every extreme that they name: `factor_rows`: entries in and above the diagonal blocks of 512 x 512 are zero. `diag_inv`: each block of 512 rows is lower triangular with a positive diagonal.
All inputs are finite; a program needn't handle non-finite values.
Results may differ from a plain program's by a relative error of at most 0.004.
Values may be sent and summed in bfloat16 or wider, within the bound.
No kernel may reach another device: no remote copies, remote signals or barrier semaphores. Data moves between devices by JAX's collectives and lax.ppermute only.
A program may use at most 320 MiB of HBM per device.

v0:
```python
import jax
import jax.numpy as jnp
from jax import lax
from jax.sharding import PartitionSpec as P

FEAT = 8192
GRID = 21


def from_behind(shard, axis, by):
    peers = lax.axis_size(axis)
    pairs = [(i, i + by) for i in range(peers) if 0 <= i + by < peers]
    return lax.ppermute(shard, axis, pairs)


def solve_chain(whitened, factor_rows, diag_inv):
    sections = lax.axis_size("rows")
    position = lax.axis_index("rows")
    rows_dev = factor_rows.shape[0]
    block_width = diag_inv.shape[1]
    offset = position * rows_dev
    carried = jnp.zeros((whitened.shape[0], factor_rows.shape[1]), jnp.float32)
    weights = jnp.zeros_like(whitened)

    def solve_own(state):
        incoming, earlier = state
        remaining = whitened - lax.dynamic_slice_in_dim(incoming, offset, rows_dev, 1)
        pieces = []
        for block_id in reversed(range(rows_dev // block_width)):
            first_col = block_id * block_width
            solved = jnp.dot(
                remaining[:, first_col : first_col + block_width],
                diag_inv,
                precision=lax.Precision.HIGHEST,
                preferred_element_type=jnp.float32,
            )
            own_columns = lax.dynamic_slice_in_dim(factor_rows, offset, rows_dev, 1)
            remaining = remaining - jnp.dot(
                solved,
                own_columns,
                precision=lax.Precision.HIGHEST,
                preferred_element_type=jnp.float32,
            )
            pieces.append(solved)
        solved_all = jnp.concatenate(pieces[::-1], axis=1)
        updated = incoming + jnp.dot(
            solved_all,
            factor_rows,
            precision=lax.Precision.HIGHEST,
            preferred_element_type=jnp.float32,
        )
        return (updated, solved_all)

    def pass_on(state):
        return state

    for section_id in range(sections):
        carried, weights = lax.cond(
            position == sections - 1 - section_id, solve_own, pass_on, (carried, weights)
        )
        if section_id + 1 < sections:
            carried = from_behind(carried, "rows", -1)
    return weights


def prior_slab(mixture, frequencies, phases, coef_slab):
    angles = (
        lax.dot_general(
            mixture,
            frequencies,
            (((0,), (0,)), ((), ())),
            precision=lax.Precision.HIGHEST,
            preferred_element_type=jnp.float32,
        )
        + phases[None, :]
    )
    features_map = (jnp.sqrt(2.0 / FEAT) * jnp.cos(angles)).astype(jnp.bfloat16)
    return lax.dot_general(
        features_map, coef_slab, (((1,), (1,)), ((), ())), preferred_element_type=jnp.float32
    )


def cross_part(mixture, observed, inv_length, weights_wire):
    squared = jnp.zeros((mixture.shape[1], observed.shape[1]), jnp.float32)
    for column in range(mixture.shape[0]):
        gap = (mixture[column][:, None] - observed[column][None, :]) * inv_length[column]
        squared = squared + gap * gap
    kernel_tile = jnp.exp(-0.5 * squared).astype(jnp.bfloat16)
    return lax.dot_general(
        kernel_tile, weights_wire, (((1,), (1,)), ((), ())), preferred_element_type=jnp.float32
    )


def body(
    whitened,
    factor_rows,
    diag_inv,
    observed,
    inv_length,
    grid_coords,
    frequencies,
    phases,
    prior_coef,
):
    coef_all = lax.all_gather(prior_coef, "cand", axis=0, tiled=True)
    weights = lax.all_gather(
        solve_chain(whitened, factor_rows, diag_inv).astype(jnp.bfloat16),
        "cand",
        axis=0,
        tiled=True,
    )
    mixture = grid_coords.astype(jnp.float32) / (GRID - 1)
    summed = prior_slab(mixture, frequencies, phases, coef_all) + cross_part(
        mixture, observed, inv_length, weights
    )
    return lax.psum_scatter(summed, "rows", scatter_dimension=1, tiled=True)


def solution(mesh):
    in_specs = (
        P("cand", "rows"),
        P("rows", None),
        P("rows", None),
        P(None, "rows"),
        P(),
        P(None, "cand"),
        P(None, "rows"),
        P("rows"),
        P("cand", "rows"),
    )
    out_specs = P("cand", "rows")
    return jax.shard_map(body, mesh=mesh, in_specs=in_specs, out_specs=out_specs, check_vma=False)
```

profile of v0, /device:TPU:1, one launch (start us, length us, event | category | flops | bytes accessed | tf_op | source)
XLA Modules:
  0.0 327.4 jit_solution(7780740695992511488)
XLA Ops:
  6.5 0.0 copy-start
  6.5 0.0 all-gather.4.cloned.1.call-start
  6.5 0.7 all-gather.4.cloned.1.call-update
  7.3 0.0 reduce-scatter.2.cloned.1.call-start
  7.3 0.6 conditional.4
  7.3 0.6 broadcast_in_dim.6
  7.9 1.3 collective-permute-start
  9.2 1.0 convert_multiply_fusion
  10.3 0.0 copy-start.3
  10.3 0.3 fusion.85
  10.6 0.8 fusion.88
  11.4 1.2 fusion.87
  12.6 2.1 fusion.89
  14.6 1.4 fusion.90
  16.1 0.0 collective-permute-done
  16.1 1.3 collective-permute-start.1
  17.4 44.7 %exponential_convert_fusion.4 = bf16[4096,512]{1,0:T(8,128)(2,1)} fusion(f32[]{:T(128)} %bitcast.66, f32[512]{0:T(512)S(1)} %bitcast.129, f32[4096]{0:T(1024)S(1)} %bitcast.107, f32[]{:T(128)} %bitcast.63, f32[512]{0:T(512)S(1)} %bitcast.130, f32[4096]{0:T(1024)S(1)} %bitcast.87, f32[]{:T(128)} %bitcast.60, f32[512]{0:T(512)S(1)} %bitcast.110, ...), kind=kLoop, calls=%fused_computation.18.clone.clone.1 | loop fusion | flops 186646528 | bytes 4599896 | tf_op jit(solution)/shard_map/dot_general | solution.py:89
  62.0 0.0 collective-permute-done.1
  62.0 0.0 copy-start.2
  62.0 0.0 copy-start.4
  62.0 0.0 copy-start.5
  62.1 1.6 collective-permute-start.2
  63.7 0.0 copy-done
  63.7 0.0 copy-done.3
  63.7 30.3 %fusion.84 = f32[4096,2048]{1,0:T(8,128)} fusion(f32[22,2048]{1,0:T(8,128)S(1)} %copy-done, s32[22,4096]{1,0:T(8,128)S(1)} %copy-done.3), kind=kOutput, calls=%fused_computation.91 | convolution fusion | flops 2214772736 | bytes 34095104 | tf_op jit(solution)/shard_map/dot_general | solution.py:68
  94.0 0.0 collective-permute-done.2
  94.0 0.0 copy-done.2
  94.0 0.0 copy-done.4
  94.0 1.2 conditional.7
  94.0 1.2 fusion.8
  95.3 0.7 convert_bitcast_fusion
  96.0 48.9 %all-gather.1 = bf16[64,4,512]{2,1,0:T(4,128)(2,1)S(1)} all-gather(bf16[1,4,512]{2,1,0:T(4,128)(2,1)S(1)} %convert_bitcast_fusion), channel_id=1, replica_groups=mesh['rows'=4,'cand'=64] {'cand'}, dimensions={0}, use_global_device_ids=true | all-gather | bytes 266240 | tf_op jit(solution)/shard_map/all_gather | solution.py:106
  144.8 0.1 reshape.26
  144.9 0.0 all-gather.4.cloned.1.call-done
  144.9 1.3 reshape.24
  146.3 0.0 copy-done.5
  146.3 0.0 copy-start.1
  146.3 114.3 %fusion.12 = f32[4096,256]{0,1:T(8,128)S(1)} fusion(bf16[256,2048]{1,0:T(8,128)(2,1)S(1)} %reshape.24, f32[4096,2048]{1,0:T(8,128)} %fusion.84, f32[2048]{0:T(1024)S(1)} %copy-done.5), kind=kOutput, calls=%fused_computation.15 | convolution fusion | flops 4320133120 | bytes 38805504 | tf_op jit(solution)/shard_map/dot_general | solution.py:78
  260.6 0.0 copy-done.1
  260.6 3.4 %convolution_add_fusion.2 = f32[4096,256]{0,1:T(8,128)} fusion(f32[4096,256]{0,1:T(8,128)S(1)} %fusion.12, bf16[256,512]{1,0:T(8,128)(2,1)S(1)} %reshape.26, bf16[4096,512]{1,0:T(8,128)(2,1)S(1)} %copy-done.1), kind=kOutput, calls=%fused_computation.19 | convolution fusion | flops 1074790400 | bytes 12845056 | tf_op jit(solution)/shard_map/dot_general | solution.py:89
  264.0 0.0 reduce-scatter.2.cloned.1.call-update
  264.0 56.5 %reduce-scatter.2.cloned.1.call-done = f32[4096,64]{0,1:T(8,128)} async-done(((f32[4096,256]{0,1:T(8,128)}), f32[4096,64]{0,1:T(8,128)}) %reduce-scatter.2.cloned.1.call-update) | async-done | bytes 1048592 | tf_op jit(solution)/shard_map/reduce_scatter | solution.py:116
  (4 shorter events, 0.0 us)
Async XLA Ops:
  6.5 57.1 %copy-start = (f32[22,2048]{1,0:T(8,128)S(1)}, f32[22,2048]{1,0:T(8,128)}, u32[]{:S(2)}) copy-start(f32[22,2048]{1,0:T(8,128)} %param.23) | copy-start | bytes 540676
  6.5 138.4 %all-gather.4.cloned.1.call-start = ((), (), s32[]{:S(2)}) async-start(), calls=%async_computation.2 | async-start | bytes 1064960 | tf_op jit(solution)/shard_map/all_gather | solution.py:105
  7.3 313.3 %reduce-scatter.2.cloned.1.call-start = ((), (), s32[]{:S(2)}) async-start(), calls=%async_computation.1 | async-start | bytes 5242880 | tf_op jit(solution)/shard_map/reduce_scatter | solution.py:116
  7.9 8.1 %collective-permute-start = (f32[4,2048]{1,0:T(4,128)S(1)}, f32[4,2048]{1,0:T(4,128)S(1)}, u32[]{:S(2)}, u32[]{:S(2)}) collective-permute-start(f32[4,2048]{1,0:T(4,128)S(1)} %get-tuple-element.77), channel_id=1, source_target_pairs={{64,0},{128,64},{192,128},{65,1},{129,65},{193,129},{66,2},{130,66... | collective-permute-start | bytes 98312 | tf_op jit(solution)/shard_map/ppermute | solution.py:13
  10.3 53.4 %copy-start.3 = (s32[22,4096]{1,0:T(8,128)S(1)}, s32[22,4096]{1,0:T(8,128)}, u32[]{:S(2)}) copy-start(s32[22,4096]{1,0:T(8,128)} %param.22) | copy-start | bytes 1081348
  16.1 45.9 %collective-permute-start.1 = (f32[4,2048]{1,0:T(4,128)S(1)}, f32[4,2048]{1,0:T(4,128)S(1)}, u32[]{:S(2)}, u32[]{:S(2)}) collective-permute-start(f32[4,2048]{1,0:T(4,128)S(1)} %get-tuple-element.79), channel_id=1, source_target_pairs={{64,0},{128,64},{192,128},{65,1},{129,65},{193,129},{66,2},{130,66... | collective-permute-start | bytes 98312 | tf_op jit(solution)/shard_map/ppermute | solution.py:13
  62.0 32.0 %copy-start.2 = (f32[512,512]{1,0:T(8,128)S(1)}, f32[512,512]{1,0:T(8,128)}, u32[]{:S(2)}) copy-start(f32[512,512]{1,0:T(8,128)} %param.19) | copy-start | bytes 3145732
  62.0 32.0 %copy-start.4 = (f32[4,512]{1,0:T(4,128)S(1)}, f32[4,512]{1,0:T(4,128)}, u32[]{:S(2)}) copy-start(f32[4,512]{1,0:T(4,128)} %param.17) | copy-start | bytes 24580
  62.0 84.2 %copy-start.5 = (f32[2048]{0:T(1024)S(1)}, f32[2048]{0:T(1024)}, u32[]{:S(2)}) copy-start(f32[2048]{0:T(1024)} %param.24) | copy-start | bytes 24580
  62.1 32.0 %collective-permute-start.2 = (f32[4,2048]{1,0:T(4,128)S(1)}, f32[4,2048]{1,0:T(4,128)S(1)}, u32[]{:S(2)}, u32[]{:S(2)}) collective-permute-start(f32[4,2048]{1,0:T(4,128)S(1)} %get-tuple-element.82), channel_id=1, source_target_pairs={{64,0},{128,64},{192,128},{65,1},{129,65},{193,129},{66,2},{130,66... | collective-permute-start | bytes 98312 | tf_op jit(solution)/shard_map/ppermute | solution.py:13
  146.3 114.3 %copy-start.1 = (bf16[4096,512]{1,0:T(8,128)(2,1)S(1)}, bf16[4096,512]{1,0:T(8,128)(2,1)}, u32[]{:S(2)}) copy-start(bf16[4096,512]{1,0:T(8,128)(2,1)} %exponential_convert_fusion.4) | copy-start | bytes 12582916
Sparse Core Ops, SparseCore 0:
  10.1 80.9 all-gather.3
  264.1 56.3 reduce-scatter.1
where the time goes:
time: 328 us; the launch traced here: 327 us
  matrix products  149 us (45%)
  waiting for transfers between devices  57.3 us (17%)
  blocking collectives  48.9 us (15%)
  other arithmetic  46.4 us (14%)
  between operations  13.6 us (4%)
  local copies, waits for them, and re-layouts  7.82 us (2%)
  starting transfers between devices  4.21 us (1%)
    dot_general x1, matrix products, prior_slab(): lax.dot_general(features_map, coef_slab, (((1,), (1,)), ((), ())), prefer...  114 us
    reduce_scatter x1, waiting for transfers between devices, body(): return lax.psum_scatter(summed, 'rows', scatter_dimension=1, tiled=True)  56.5 us
    all_gather x1, blocking collectives, body(): lax.all_gather(solve_chain(whitened, factor_rows, diag_inv).astype(jnp.bf...  48.9 us
    dot_general x1, other arithmetic, cross_part(): lax.dot_general(kernel_tile, weights_wire, (((1,), (1,)), ((), ())), pref...  44.7 us
    dot_general x1, matrix products, prior_slab(): lax.dot_general(mixture, frequencies, (((0,), (0,)), ((), ())), precision...  30.3 us
  transfers between devices with their start and end apart: 5, of which 1 were waited for; matrix products, arithmetic and copies ran while one was open for 26% of the time, Pallas kernels for 0%

commit v1 on v0

--- a/solution.py
+++ b/solution.py
@@ -103,12 +103,11 @@
     prior_coef,
 ):
     coef_all = lax.all_gather(prior_coef, "cand", axis=0, tiled=True)
-    weights = lax.all_gather(
-        solve_chain(whitened, factor_rows, diag_inv).astype(jnp.bfloat16),
-        "cand",
-        axis=0,
-        tiled=True,
-    )
+    block = solve_chain(whitened, factor_rows, diag_inv).astype(jnp.bfloat16)
+    count = lax.axis_size("cand")
+    blocks = jnp.stack([block for _ in range(count)])
+    blocks = lax.all_to_all(blocks, "cand", split_axis=0, concat_axis=0)
+    weights = jnp.concatenate(blocks, axis=0)
     mixture = grid_coords.astype(jnp.float32) / (GRID - 1)
     summed = prior_slab(mixture, frequencies, phases, coef_all) + cross_part(
         mixture, observed, inv_length, weights

time: 328 us -> 307 us (0.936)
  blocking collectives: 48.9 us -> 0 us
  starting transfers between devices: 4.21 us -> 17.7 us
  waiting for transfers between devices: 57.3 us -> 70.2 us
    all_gather x1 -> x0, blocking collectives: 48.9 us -> none  [body(): lax.all_gather(solve_chain(whitened, factor_rows, diag_inv).astype(jnp.bf...]
    all_to_all x0 -> x1, starting transfers between devices: none -> 13.7 us  [body(): blocks = lax.all_to_all(blocks, 'cand', split_axis=0, concat_axis=0)]
    reduce_scatter x1, waiting for transfers between devices: 56.5 us -> 65.4 us  [body(): return lax.psum_scatter(summed, 'rows', scatter_dimension=1, tiled=True)]
    ppermute x3, waiting for transfers between devices: 0.01 us -> 4 us  [from_behind(): return lax.ppermute(shard, axis, pairs)]
  transfers between devices with their start and end apart: 5 -> 6, of which waited for: 1 -> 2; matrix products, arithmetic and copies ran while one was open for 26% -> 28% of each run, Pallas kernels for 0% -> 0%
where the time goes in v1:
time: 307 us; the launch traced here: 306 us
  matrix products  150 us (49%)
  waiting for transfers between devices  70.2 us (23%)
  other arithmetic  46.4 us (15%)
  starting transfers between devices  17.7 us (6%)
  between operations  13.6 us (4%)
  local copies, waits for them, and re-layouts  7.78 us (3%)
    dot_general x1, matrix products, prior_slab(): lax.dot_general(features_map, coef_slab, (((1,), (1,)), ((), ())), prefer...  114 us
    reduce_scatter x1, waiting for transfers between devices, body(): return lax.psum_scatter(summed, 'rows', scatter_dimension=1, tiled=True)  65.4 us
    dot_general x1, other arithmetic, cross_part(): lax.dot_general(kernel_tile, weights_wire, (((1,), (1,)), ((), ())), pref...  44.6 us
    dot_general x1, matrix products, prior_slab(): lax.dot_general(mixture, frequencies, (((0,), (0,)), ((), ())), precision...  30.2 us
    all_to_all x1, starting transfers between devices, body(): blocks = lax.all_to_all(blocks, 'cand', split_axis=0, concat_axis=0)  13.7 us
  transfers between devices with their start and end apart: 6, of which 2 were waited for; matrix products, arithmetic and copies ran while one was open for 28% of the time, Pallas kernels for 0%

profile of v1, /device:TPU:1, one launch (start us, length us, event | category | flops | bytes accessed | tf_op | source)
XLA Modules:
  0.0 306.0 jit_solution(5156806620968819691)
XLA Ops:
  6.5 0.0 copy-start
  6.5 0.0 copy-start.3
  6.5 0.0 all-gather.3.cloned.1.call-start
  6.5 0.7 all-gather.3.cloned.1.call-update
  7.3 0.6 conditional.4
  7.3 0.6 broadcast_in_dim.6
  7.9 1.3 collective-permute-start
  9.2 1.0 convert_multiply_fusion
  10.3 0.3 fusion.85
  10.6 0.8 fusion.88
  11.4 1.2 fusion.87
  12.5 2.0 fusion.89
  14.6 0.0 collective-permute-done
  14.6 0.0 copy-start.2
  14.6 1.4 collective-permute-start.1
  16.0 0.0 copy-done.3
  16.1 0.6 fusion.90
  16.7 4.0 %collective-permute-done.1 = f32[4,2048]{1,0:T(4,128)S(1)} collective-permute-done((f32[4,2048]{1,0:T(4,128)S(1)}, f32[4,2048]{1,0:T(4,128)S(1)}, u32[]{:S(2)}, u32[]{:S(2)}) %collective-permute-start.1) | collective-permute-done | bytes 32800 | tf_op jit(solution)/shard_map/ppermute | solution.py:13
  20.7 1.3 collective-permute-start.2
  22.0 44.6 %exponential_convert_fusion.4 = bf16[4096,512]{1,0:T(8,128)(2,1)} fusion(f32[]{:T(128)} %bitcast.66, f32[512]{0:T(512)S(1)} %bitcast.127, f32[4096]{0:T(1024)S(1)} %bitcast.105, f32[]{:T(128)} %bitcast.63, f32[512]{0:T(512)S(1)} %bitcast.128, f32[4096]{0:T(1024)S(1)} %bitcast.85, f32[]{:T(128)} %bitcast.60, f32[512]{0:T(512)S(1)} %bitcast.108, ...), kind=kLoop, calls=%fused_computation.18.clone.clone.1 | loop fusion | flops 186646528 | bytes 4599896 | tf_op jit(solution)/shard_map/dot_general | solution.py:89
  66.6 0.0 collective-permute-done.2
  66.6 2.5 conditional.7
  66.6 2.5 fusion.8
  69.1 0.7 convert_element_type.31
  69.8 0.8 stack.2
  70.5 13.7 %all-to-all-start = ((bf16[64,4,512]{2,1,0:T(4,128)(2,1)}), bf16[64,4,512]{2,1,0:T(4,128)(2,1)S(1)}, u32[]{:S(2)}, u32[]{:S(2)}) async-start(bf16[64,4,512]{2,1,0:T(4,128)(2,1)} %stack.2), calls=%async_computation | async-start | bytes 524288 | tf_op jit(solution)/shard_map/all_to_all | solution.py:109
  84.2 0.0 copy-start.4
  84.2 0.0 reduce-scatter.2.cloned.1.call-start
  84.3 0.0 copy-done
  84.3 0.0 copy-done.2
  84.3 30.2 %fusion.84 = f32[4096,2048]{1,0:T(8,128)} fusion(f32[22,2048]{1,0:T(8,128)S(1)} %copy-done, s32[22,4096]{1,0:T(8,128)S(1)} %copy-done.2), kind=kOutput, calls=%fused_computation.90 | convolution fusion | flops 2214772736 | bytes 34095104 | tf_op jit(solution)/shard_map/dot_general | solution.py:68
  114.5 0.0 all-to-all-done
  114.5 0.1 reshape.28
  114.5 0.0 all-gather.3.cloned.1.call-done
  114.6 1.3 reshape.30
  115.9 0.0 copy-done.4
  115.9 0.0 copy-start.1
  115.9 114.4 %fusion.12 = f32[4096,256]{0,1:T(8,128)S(1)} fusion(bf16[256,2048]{1,0:T(8,128)(2,1)S(1)} %reshape.30, f32[4096,2048]{1,0:T(8,128)} %fusion.84, f32[2048]{0:T(1024)S(1)} %copy-done.4), kind=kOutput, calls=%fused_computation.15 | convolution fusion | flops 4320133120 | bytes 38805504 | tf_op jit(solution)/shard_map/dot_general | solution.py:78
  230.3 0.0 copy-done.1
  230.3 3.4 %convolution_add_fusion.2 = f32[4096,256]{0,1:T(8,128)} fusion(f32[4096,256]{0,1:T(8,128)S(1)} %fusion.12, bf16[256,512]{1,0:T(8,128)(2,1)S(1)} %reshape.28, bf16[4096,512]{1,0:T(8,128)(2,1)S(1)} %copy-done.1), kind=kOutput, calls=%fused_computation.19 | convolution fusion | flops 1074790400 | bytes 12845056 | tf_op jit(solution)/shard_map/dot_general | solution.py:89
  233.7 0.0 reduce-scatter.2.cloned.1.call-update
  233.8 65.4 %reduce-scatter.2.cloned.1.call-done = f32[4096,64]{0,1:T(8,128)} async-done(((f32[4096,256]{0,1:T(8,128)}), f32[4096,64]{0,1:T(8,128)}) %reduce-scatter.2.cloned.1.call-update) | async-done | bytes 1048592 | tf_op jit(solution)/shard_map/reduce_scatter | solution.py:115
  (4 shorter events, 0.1 us)
Async XLA Ops:
  6.5 77.7 %copy-start = (f32[22,2048]{1,0:T(8,128)S(1)}, f32[22,2048]{1,0:T(8,128)}, u32[]{:S(2)}) copy-start(f32[22,2048]{1,0:T(8,128)} %param.23) | copy-start | bytes 540676
  6.5 9.5 %copy-start.3 = (f32[22]{0:T(128)S(1)}, f32[22]{0:T(128)}, u32[]{:S(2)}) copy-start(f32[22]{0:T(128)} %param.21) | copy-start | bytes 268
  6.5 108.0 %all-gather.3.cloned.1.call-start = ((), (), s32[]{:S(2)}) async-start(), calls=%async_computation.3 | async-start | bytes 1064960 | tf_op jit(solution)/shard_map/all_gather | solution.py:105
  7.9 6.7 %collective-permute-start = (f32[4,2048]{1,0:T(4,128)S(1)}, f32[4,2048]{1,0:T(4,128)S(1)}, u32[]{:S(2)}, u32[]{:S(2)}) collective-permute-start(f32[4,2048]{1,0:T(4,128)S(1)} %get-tuple-element.77), channel_id=1, source_target_pairs={{64,0},{128,64},{192,128},{65,1},{129,65},{193,129},{66,2},{130,66... | collective-permute-start | bytes 98312 | tf_op jit(solution)/shard_map/ppermute | solution.py:13
  14.6 69.7 %copy-start.2 = (s32[22,4096]{1,0:T(8,128)S(1)}, s32[22,4096]{1,0:T(8,128)}, u32[]{:S(2)}) copy-start(s32[22,4096]{1,0:T(8,128)} %param.22) | copy-start | bytes 1081348
  14.6 6.1 %collective-permute-start.1 = (f32[4,2048]{1,0:T(4,128)S(1)}, f32[4,2048]{1,0:T(4,128)S(1)}, u32[]{:S(2)}, u32[]{:S(2)}) collective-permute-start(f32[4,2048]{1,0:T(4,128)S(1)} %get-tuple-element.79), channel_id=1, source_target_pairs={{64,0},{128,64},{192,128},{65,1},{129,65},{193,129},{66,2},{130,66... | collective-permute-start | bytes 98312 | tf_op jit(solution)/shard_map/ppermute | solution.py:13
  20.7 45.9 %collective-permute-start.2 = (f32[4,2048]{1,0:T(4,128)S(1)}, f32[4,2048]{1,0:T(4,128)S(1)}, u32[]{:S(2)}, u32[]{:S(2)}) collective-permute-start(f32[4,2048]{1,0:T(4,128)S(1)} %get-tuple-element.82), channel_id=1, source_target_pairs={{64,0},{128,64},{192,128},{65,1},{129,65},{193,129},{66,2},{130,66... | collective-permute-start | bytes 98312 | tf_op jit(solution)/shard_map/ppermute | solution.py:13
  70.5 43.9 %all-to-all-start = ((bf16[64,4,512]{2,1,0:T(4,128)(2,1)}), bf16[64,4,512]{2,1,0:T(4,128)(2,1)S(1)}, u32[]{:S(2)}, u32[]{:S(2)}) async-start(bf16[64,4,512]{2,1,0:T(4,128)(2,1)} %stack.2), calls=%async_computation | async-start | bytes 524288 | tf_op jit(solution)/shard_map/all_to_all | solution.py:109
  84.2 31.7 %copy-start.4 = (f32[2048]{0:T(1024)S(1)}, f32[2048]{0:T(1024)}, u32[]{:S(2)}) copy-start(f32[2048]{0:T(1024)} %param.24) | copy-start | bytes 24580
  84.2 215.0 %reduce-scatter.2.cloned.1.call-start = ((), (), s32[]{:S(2)}) async-start(), calls=%async_computation.2 | async-start | bytes 5242880 | tf_op jit(solution)/shard_map/reduce_scatter | solution.py:115
  115.9 114.4 %copy-start.1 = (bf16[4096,512]{1,0:T(8,128)(2,1)S(1)}, bf16[4096,512]{1,0:T(8,128)(2,1)}, u32[]{:S(2)}) copy-start(bf16[4096,512]{1,0:T(8,128)(2,1)} %exponential_convert_fusion.4) | copy-start | bytes 12582916
Sparse Core Ops, SparseCore 0:
  10.1 81.3 all-gather.2
  233.9 65.2 reduce-scatter.1
